TPU v7x, 256 devices: a whole 4x4x8 slice. The times are simulated.
256 devices in a mesh: feat: 64 (over x, z, core), node: 4 (over y).
Axes of the slice: x: 4, y: 4, z: 8, core: 2. Of those that a mesh axis runs over, the one named last changes fastest.
Arguments:
- features: bfloat16 [32768, 1024], P(None, 'feat'), may hold values from -6 to 6
- w_self: bfloat16 [1024, 256], P('feat'), may hold values from -0.1875 to 0.1875
- w_neigh: bfloat16 [1024, 256], P('feat'), may hold values from -0.75 to 0.75
- bias: float32 [256], replicated, may hold values from -3 to 3
- d_out: bfloat16 [32768, 256], P(('node', 'feat')), may hold values from -6 to 6
- nbr_ids: int32 [256, 16], P('node'), may hold values from 0 to 255, as said below
- nbr_count: int32 [256], P('node'), may hold values from 1 to 16, as said below
- tiles: int32 [256, 16, 8, 128], P('node'), may hold values from 0 to 65535, as said below
Outputs:
- activated: bfloat16 [32768, 256], P(('node', 'feat'))
- grad_features: float32 [32768, 1024], P('node', 'feat')
- grad_self: float32 [1024, 256], P('feat')
- grad_neigh: float32 [1024, 256], P('feat')
Inputs may be any that keep to these rules, and one draw needn't show every extreme that they name: `nbr_ids`: the ids of one block row are distinct; only the first nbr_count slots of a row are live, the others hold ids and tiles that must be ignored. `nbr_count`: some block row of every draw has exactly 16 live slots. `tiles`: bits for destination rows 128 and above are zero; some destination nodes have no edges at all.
All inputs are finite; a program needn't handle non-finite values.
Results may differ from a plain program's by a relative error of at most 0.0075.
Values may be sent and summed in bfloat16 or wider, within the bound.
A program may use at most 64 MiB of HBM per device.

v0:
```python
import math
import jax
import jax.numpy as jnp
from jax import lax
from jax.sharding import PartitionSpec as P


def unpack(packed):
    shifts = jnp.arange(16, dtype=jnp.int32)
    bit_planes = jnp.bitwise_and(jnp.right_shift(packed[..., :, None, :], shifts[:, None]), 1)
    flat_shape = packed.shape[:-2] + (packed.shape[-2] * 16, packed.shape[-1])
    return bit_planes.reshape(flat_shape)


def shards(features, w_self, w_neigh, bias, d_out, nbr_ids, nbr_count, tiles):
    node_total = features.shape[0]
    feat_cols = features.shape[1]
    block_size = tiles.shape[3]
    blocks_here = nbr_ids.shape[0]
    group_rows = blocks_here * block_size
    all_blocks = node_total // block_size
    slot_total = nbr_ids.shape[1]
    node_group = lax.axis_index("node")
    blocked = features.reshape(all_blocks, block_size, feat_cols)

    def slot_tiles(slot_idx):
        packed = lax.dynamic_index_in_dim(tiles, slot_idx, 1, keepdims=False)
        block_ids = lax.dynamic_index_in_dim(nbr_ids, slot_idx, 1, keepdims=False)
        live_mask = (slot_idx < nbr_count).astype(jnp.float32)
        adjacency = unpack(packed).astype(jnp.bfloat16)
        return (adjacency, block_ids, live_mask)

    def forward_slot(slot_idx, state_pair):
        neigh_sum, degree = state_pair
        adjacency, block_ids, live_mask = slot_tiles(slot_idx)
        source = blocked[block_ids]
        product = jnp.einsum("bij,bjc->bic", adjacency, source, preferred_element_type=jnp.float32)
        neigh_sum = neigh_sum + product * live_mask[:, None, None]
        degree = degree + jnp.sum(adjacency, axis=2, dtype=jnp.float32) * live_mask[:, None]
        return (neigh_sum, degree)

    neigh_sum, degree = lax.fori_loop(
        0,
        slot_total,
        forward_slot,
        (
            jnp.zeros((blocks_here, block_size, feat_cols), jnp.float32),
            jnp.zeros((blocks_here, block_size), jnp.float32),
        ),
    )
    denom = jnp.maximum(degree, 1.0)
    neigh_mean = (neigh_sum / denom[..., None]).astype(jnp.bfloat16).reshape(group_rows, feat_cols)
    own_rows = lax.dynamic_slice_in_dim(features, node_group * group_rows, group_rows, 0)
    pre_act = (
        lax.psum_scatter(
            jnp.dot(own_rows, w_self, preferred_element_type=jnp.float32)
            + jnp.dot(neigh_mean, w_neigh, preferred_element_type=jnp.float32),
            "feat",
            scatter_dimension=0,
            tiled=True,
        )
        + bias
    )
    activated = jax.nn.elu(pre_act).astype(jnp.bfloat16)
    elu_slope = jnp.where(pre_act > 0, 1.0, jnp.exp(jnp.minimum(pre_act, 0.0)))
    dpre = (d_out.astype(jnp.float32) * elu_slope).astype(jnp.bfloat16)
    dpre_group = lax.all_gather(dpre, "feat", axis=0, tiled=True)
    part_self = lax.dot_general(
        own_rows, dpre_group, (((0,), (0,)), ((), ())), preferred_element_type=jnp.float32
    )
    part_neigh = lax.dot_general(
        neigh_mean, dpre_group, (((0,), (0,)), ((), ())), preferred_element_type=jnp.float32
    )
    sum_self, sum_neigh = lax.psum((part_self, part_neigh), "node")
    d_self = lax.dot_general(
        dpre_group, w_self, (((1,), (1,)), ((), ())), preferred_element_type=jnp.float32
    ).astype(jnp.bfloat16)
    d_neigh = lax.dot_general(
        dpre_group, w_neigh, (((1,), (1,)), ((), ())), preferred_element_type=jnp.float32
    ).astype(jnp.bfloat16)
    grad_scale = 1.0 / math.sqrt(node_total)
    grad_self = sum_self * grad_scale
    grad_neigh = sum_neigh * grad_scale
    d_scaled = (
        d_neigh.astype(jnp.float32).reshape(blocks_here, block_size, feat_cols) / denom[..., None]
    ).astype(jnp.bfloat16)

    def backward_slot(slot_idx, grad_all):
        adjacency, block_ids, live_mask = slot_tiles(slot_idx)
        product = jnp.einsum(
            "bij,bic->bjc", adjacency, d_scaled, preferred_element_type=jnp.float32
        )
        return grad_all.at[block_ids].add(product * live_mask[:, None, None])

    grad_all = lax.fori_loop(
        0, slot_total, backward_slot, jnp.zeros((all_blocks, block_size, feat_cols), jnp.float32)
    )
    flat_grad = grad_all.reshape(node_total, feat_cols)
    group_part = lax.dynamic_slice_in_dim(flat_grad, node_group * group_rows, group_rows, 0)
    flat_grad = lax.dynamic_update_slice_in_dim(
        flat_grad, group_part + d_self.astype(jnp.float32), node_group * group_rows, 0
    )
    grad_features = lax.psum_scatter(flat_grad, "node", scatter_dimension=0, tiled=True)
    return (activated, grad_features, grad_self, grad_neigh)


def solution(mesh):
    placed = (
        P(None, "feat"),
        P("feat", None),
        P("feat", None),
        P(),
        P(("node", "feat"), None),
        P("node", None),
        P("node"),
        P("node", None, None, None),
    )
    return jax.shard_map(
        shards,
        mesh=mesh,
        in_specs=placed,
        out_specs=(P(("node", "feat"), None), P("node", "feat"), P("feat", None), P("feat", None)),
        check_vma=False,
    )
```

profile of v0, /device:TPU:1, one launch (start us, length us, event | category | flops | bytes accessed | tf_op | source)
XLA Modules:
  0.0 586.5 jit_solution(15753192361563251253)
XLA Ops:
  8.6 4.6 copy.24
  13.2 101.6 %while.30 = (s32[]{:T(128)}, f32[64,128,16]{1,2,0:T(8,128)S(1)}, f32[64,128]{0,1:T(8,128)S(1)}, s32[64,16,8,128]{3,2,0,1:T(8,128)}, s32[64,16]{0,1:T(8,128)}, /*...) while((s32[]{:T(128)}, f32[64,128,16]{1,2,0:T(8,128)S(1)}, ...), condition=%wide.region_2.3_spmd.clone, body=%wide.region_0.2_spmd.clone.sunk | while | flops 42353984 | bytes 7282812 | solution.py:42
  18.3 1.2 fusion.66
  114.9 1.3 fusion.22
  116.2 4.5 convolution_add_fusion
  120.8 150.6 %reduce-scatter.3.cloned.1.call-done = f32[128,256]{1,0:T(8,128)} async-done(((f32[8192,256]{1,0:T(8,128)}), f32[128,256]{1,0:T(8,128)}) %reduce-scatter.3.cloned.1.call-update) | async-done | bytes 131088 | tf_op jit(solution)/shard_map/reduce_scatter | solution.py:55
  271.5 1.6 fusion.27
  273.2 84.5 %all-gather.2.cloned.1.call-done = bf16[8192,256]{1,0:T(8,128)(2,1)} async-done(((bf16[128,256]{1,0:T(8,128)(2,1)}), bf16[8192,256]{1,0:T(8,128)(2,1)}) %all-gather.2.cloned.1.call-update) | async-done | bytes 4194320 | tf_op jit(solution)/shard_map/all_gather | solution.py:67
  357.6 3.4 fusion.12
  361.1 1.5 broadcast_in_dim.47
  362.6 181.3 %while.29 = (s32[]{:T(128)}, f32[256,128,16]{1,2,0:T(8,128)}, s32[64,16]{0,1:T(8,128)}, s32[64,16,8,128]{3,2,0,1:T(8,128)}, bf16[64,128,16]{1,2,0:T(8,128)(2,1)S(1)}, /*index=5*/s32[64]{0:T(128)}, s32[]{:T(128)}) while((s32[]{:T(128)}, f32[256,128,16]{1,2,0:T(8,128)}, s32[64,16]{0,1:T(8,128)}, s32[64,16,8,128]{3,2,0,1:T(8,128)}, ...), condition=%wide.region_6.7_spmd, body=%wide.region_4.6_spmd.sunk | while | flops 36962624 | bytes 7343713 | solution.py:95
  366.4 7.5 %scatter_fusion = f32[256,128,16]{1,2,0:T(8,128)} fusion(f32[256,128,16]{1,2,0:T(8,128)} %get-tuple-element.451, s32[64]{0:T(128)S(1)} %fusion.60, f32[64,128,16]{1,2,0:T(8,128)S(1)} %convolution_multiply_fusion.3), kind=kCustom, calls=%fused_computation.1.clone.1 | custom fusion | flops 131072 | bytes 1573120 | tf_op jit(solution)/shard_map/while/body/eval_jaxpr/scatter-add | solution.py:93
  377.7 7.5 %scatter_fusion = f32[256,128,16]{1,2,0:T(8,128)} fusion(f32[256,128,16]{1,2,0:T(8,128)} %get-tuple-element.451, s32[64]{0:T(128)S(1)} %fusion.60, f32[64,128,16]{1,2,0:T(8,128)S(1)} %convolution_multiply_fusion.3), kind=kCustom, calls=%fused_computation.1.clone.1 | custom fusion | flops 131072 | bytes 1573120 | tf_op jit(solution)/shard_map/while/body/eval_jaxpr/scatter-add | solution.py:93
  389.0 7.5 %scatter_fusion = f32[256,128,16]{1,2,0:T(8,128)} fusion(f32[256,128,16]{1,2,0:T(8,128)} %get-tuple-element.451, s32[64]{0:T(128)S(1)} %fusion.60, f32[64,128,16]{1,2,0:T(8,128)S(1)} %convolution_multiply_fusion.3), kind=kCustom, calls=%fused_computation.1.clone.1 | custom fusion | flops 131072 | bytes 1573120 | tf_op jit(solution)/shard_map/while/body/eval_jaxpr/scatter-add | solution.py:93
  400.4 7.5 %scatter_fusion = f32[256,128,16]{1,2,0:T(8,128)} fusion(f32[256,128,16]{1,2,0:T(8,128)} %get-tuple-element.451, s32[64]{0:T(128)S(1)} %fusion.60, f32[64,128,16]{1,2,0:T(8,128)S(1)} %convolution_multiply_fusion.3), kind=kCustom, calls=%fused_computation.1.clone.1 | custom fusion | flops 131072 | bytes 1573120 | tf_op jit(solution)/shard_map/while/body/eval_jaxpr/scatter-add | solution.py:93
  411.7 7.5 %scatter_fusion = f32[256,128,16]{1,2,0:T(8,128)} fusion(f32[256,128,16]{1,2,0:T(8,128)} %get-tuple-element.451, s32[64]{0:T(128)S(1)} %fusion.60, f32[64,128,16]{1,2,0:T(8,128)S(1)} %convolution_multiply_fusion.3), kind=kCustom, calls=%fused_computation.1.clone.1 | custom fusion | flops 131072 | bytes 1573120 | tf_op jit(solution)/shard_map/while/body/eval_jaxpr/scatter-add | solution.py:93
  423.0 7.5 %scatter_fusion = f32[256,128,16]{1,2,0:T(8,128)} fusion(f32[256,128,16]{1,2,0:T(8,128)} %get-tuple-element.451, s32[64]{0:T(128)S(1)} %fusion.60, f32[64,128,16]{1,2,0:T(8,128)S(1)} %convolution_multiply_fusion.3), kind=kCustom, calls=%fused_computation.1.clone.1 | custom fusion | flops 131072 | bytes 1573120 | tf_op jit(solution)/shard_map/while/body/eval_jaxpr/scatter-add | solution.py:93
  434.4 7.5 %scatter_fusion = f32[256,128,16]{1,2,0:T(8,128)} fusion(f32[256,128,16]{1,2,0:T(8,128)} %get-tuple-element.451, s32[64]{0:T(128)S(1)} %fusion.60, f32[64,128,16]{1,2,0:T(8,128)S(1)} %convolution_multiply_fusion.3), kind=kCustom, calls=%fused_computation.1.clone.1 | custom fusion | flops 131072 | bytes 1573120 | tf_op jit(solution)/shard_map/while/body/eval_jaxpr/scatter-add | solution.py:93
  445.7 7.5 %scatter_fusion = f32[256,128,16]{1,2,0:T(8,128)} fusion(f32[256,128,16]{1,2,0:T(8,128)} %get-tuple-element.451, s32[64]{0:T(128)S(1)} %fusion.60, f32[64,128,16]{1,2,0:T(8,128)S(1)} %convolution_multiply_fusion.3), kind=kCustom, calls=%fused_computation.1.clone.1 | custom fusion | flops 131072 | bytes 1573120 | tf_op jit(solution)/shard_map/while/body/eval_jaxpr/scatter-add | solution.py:93
  457.0 7.5 %scatter_fusion = f32[256,128,16]{1,2,0:T(8,128)} fusion(f32[256,128,16]{1,2,0:T(8,128)} %get-tuple-element.451, s32[64]{0:T(128)S(1)} %fusion.60, f32[64,128,16]{1,2,0:T(8,128)S(1)} %convolution_multiply_fusion.3), kind=kCustom, calls=%fused_computation.1.clone.1 | custom fusion | flops 131072 | bytes 1573120 | tf_op jit(solution)/shard_map/while/body/eval_jaxpr/scatter-add | solution.py:93
  468.4 7.5 %scatter_fusion = f32[256,128,16]{1,2,0:T(8,128)} fusion(f32[256,128,16]{1,2,0:T(8,128)} %get-tuple-element.451, s32[64]{0:T(128)S(1)} %fusion.60, f32[64,128,16]{1,2,0:T(8,128)S(1)} %convolution_multiply_fusion.3), kind=kCustom, calls=%fused_computation.1.clone.1 | custom fusion | flops 131072 | bytes 1573120 | tf_op jit(solution)/shard_map/while/body/eval_jaxpr/scatter-add | solution.py:93
  479.7 7.5 %scatter_fusion = f32[256,128,16]{1,2,0:T(8,128)} fusion(f32[256,128,16]{1,2,0:T(8,128)} %get-tuple-element.451, s32[64]{0:T(128)S(1)} %fusion.60, f32[64,128,16]{1,2,0:T(8,128)S(1)} %convolution_multiply_fusion.3), kind=kCustom, calls=%fused_computation.1.clone.1 | custom fusion | flops 131072 | bytes 1573120 | tf_op jit(solution)/shard_map/while/body/eval_jaxpr/scatter-add | solution.py:93
  491.0 7.5 %scatter_fusion = f32[256,128,16]{1,2,0:T(8,128)} fusion(f32[256,128,16]{1,2,0:T(8,128)} %get-tuple-element.451, s32[64]{0:T(128)S(1)} %fusion.60, f32[64,128,16]{1,2,0:T(8,128)S(1)} %convolution_multiply_fusion.3), kind=kCustom, calls=%fused_computation.1.clone.1 | custom fusion | flops 131072 | bytes 1573120 | tf_op jit(solution)/shard_map/while/body/eval_jaxpr/scatter-add | solution.py:93
  502.4 7.5 %scatter_fusion = f32[256,128,16]{1,2,0:T(8,128)} fusion(f32[256,128,16]{1,2,0:T(8,128)} %get-tuple-element.451, s32[64]{0:T(128)S(1)} %fusion.60, f32[64,128,16]{1,2,0:T(8,128)S(1)} %convolution_multiply_fusion.3), kind=kCustom, calls=%fused_computation.1.clone.1 | custom fusion | flops 131072 | bytes 1573120 | tf_op jit(solution)/shard_map/while/body/eval_jaxpr/scatter-add | solution.py:93
  513.7 7.5 %scatter_fusion = f32[256,128,16]{1,2,0:T(8,128)} fusion(f32[256,128,16]{1,2,0:T(8,128)} %get-tuple-element.451, s32[64]{0:T(128)S(1)} %fusion.60, f32[64,128,16]{1,2,0:T(8,128)S(1)} %convolution_multiply_fusion.3), kind=kCustom, calls=%fused_computation.1.clone.1 | custom fusion | flops 131072 | bytes 1573120 | tf_op jit(solution)/shard_map/while/body/eval_jaxpr/scatter-add | solution.py:93
  525.0 7.5 %scatter_fusion = f32[256,128,16]{1,2,0:T(8,128)} fusion(f32[256,128,16]{1,2,0:T(8,128)} %get-tuple-element.451, s32[64]{0:T(128)S(1)} %fusion.60, f32[64,128,16]{1,2,0:T(8,128)S(1)} %convolution_multiply_fusion.3), kind=kCustom, calls=%fused_computation.1.clone.1 | custom fusion | flops 131072 | bytes 1573120 | tf_op jit(solution)/shard_map/while/body/eval_jaxpr/scatter-add | solution.py:93
  536.4 7.5 %scatter_fusion = f32[256,128,16]{1,2,0:T(8,128)} fusion(f32[256,128,16]{1,2,0:T(8,128)} %get-tuple-element.451, s32[64]{0:T(128)S(1)} %fusion.60, f32[64,128,16]{1,2,0:T(8,128)S(1)} %convolution_multiply_fusion.3), kind=kCustom, calls=%fused_computation.1.clone.1 | custom fusion | flops 131072 | bytes 1573120 | tf_op jit(solution)/shard_map/while/body/eval_jaxpr/scatter-add | solution.py:93
  543.9 3.2 copy_bitcast_fusion
  547.1 3.0 fusion.10
  550.1 3.0 fusion.20
  554.2 14.9 %all-reduce = (f32[16,256]{1,0:T(8,128)S(1)}, f32[16,256]{1,0:T(8,128)S(1)}) all-reduce(f32[16,256]{1,0:T(8,128)S(1)} %fusion.20, f32[16,256]{1,0:T(8,128)S(1)} %fusion.14), channel_id=1, replica_groups=mesh['feat'=64,'node'=4] {'node'}, use_global_device_ids=true, to_apply=%region_8.9 | all-reduce | flops 8192 | bytes 65536 | tf_op jit(solution)/shard_map/psum | solution.py:74
  569.7 10.2 %reduce-scatter.5.cloned.1.call-done = f32[8192,16]{0,1:T(8,128)} async-done(((f32[32768,16]{0,1:T(8,128)}), f32[8192,16]{0,1:T(8,128)}) %reduce-scatter.5.cloned.1.call-update) | async-done | bytes 524304 | tf_op jit(solution)/shard_map/reduce_scatter | solution.py:103
  (331 shorter events, 164.1 us)
Async XLA Ops:
  7.2 1.2 copy-start
  7.2 264.3 %reduce-scatter.3.cloned.1.call-start = ((), (), s32[]{:S(2)}) async-start(), calls=%async_computation.2 | async-start | bytes 8519680 | tf_op jit(solution)/shard_map/reduce_scatter | solution.py:55
  13.2 101.7 %copy-start.5 = (bf16[16,256]{1,0:T(8,128)(2,1)S(1)}, bf16[16,256]{1,0:T(8,128)(2,1)}, u32[]{:S(2)}) copy-start(bf16[16,256]{1,0:T(8,128)(2,1)} %param.13) | copy-start | bytes 24580
  114.9 1.3 copy-start.4
  120.7 150.7 %copy-start.3 = (bf16[128,256]{1,0:T(8,128)(2,1)S(1)}, bf16[128,256]{1,0:T(8,128)(2,1)}, u32[]{:S(2)}) copy-start(bf16[128,256]{1,0:T(8,128)(2,1)} %param.16) | copy-start | bytes 196612
  120.7 150.7 %copy-start.6 = (f32[256]{0:T(256)S(1)}, f32[256]{0:T(256)}, u32[]{:S(2)}) copy-start(f32[256]{0:T(256)} %param.15) | copy-start | bytes 3076
  120.8 236.9 %all-gather.2.cloned.1.call-start = ((), (), s32[]{:S(2)}) async-start(), calls=%async_computation.3 | async-start | bytes 4259840 | tf_op jit(solution)/shard_map/all_gather | solution.py:67
  273.1 306.8 %reduce-scatter.5.cloned.1.call-start = ((), (), s32[]{:S(2)}) async-start(), calls=%async_computation.4 | async-start | bytes 2621440 | tf_op jit(solution)/shard_map/reduce_scatter | solution.py:103
  543.9 3.2 copy-start.1
  550.1 3.5 copy-start.2
Sparse Core Ops, SparseCore 0:
  120.9 150.5 reduce-scatter.2
  275.2 82.3 all-gather.1
  550.2 29.6 reduce-scatter.4
where the time goes:
time: 592 us; the launch traced here: 586 us
  waiting for transfers between devices  245 us (41%)
  other arithmetic  209 us (35%)
  local copies, waits for them, and re-layouts  57 us (10%)
  matrix products  45.7 us (8%)
  blocking collectives  14.9 us (3%)
  between operations  13.8 us (2%)
    reduce_scatter x1, waiting for transfers between devices, shards(): lax.psum_scatter(jnp.dot(own_rows, w_self, preferred_element_type=jnp.flo...  151 us
    scatter-add x16, other arithmetic, backward_slot(): return grad_all.at[block_ids].add(product * live_mask[:, None, None])  120 us
    all_gather x1, waiting for transfers between devices, shards(): dpre_group = lax.all_gather(dpre, 'feat', axis=0, tiled=True)  84.5 us
    shift_right_arithmetic x96, local copies, waits for them, and re-layouts, unpack(): jnp.right_shift(packed[..., :, None, :], shifts[:, None])  33.8 us
    convert_element_type x32, other arithmetic, slot_tiles(): adjacency = unpack(packed).astype(jnp.bfloat16)  23.8 us
    convert_element_type x32, other arithmetic, slot_tiles(): live_mask = (slot_idx < nbr_count).astype(jnp.float32)  21.2 us
    dot_general x16, matrix products, forward_slot(): jnp.einsum('bij,bjc->bic', adjacency, source, preferred_element_type=jnp....  19.2 us
    reduce_sum x16, other arithmetic, forward_slot(): jnp.sum(adjacency, axis=2, dtype=jnp.float32) * live_mask[:, None]  18.5 us
  transfers between devices with their start and end apart: 3, of which 3 were waited for; matrix products, arithmetic and copies ran while one was open for 1% of the time, Pallas kernels for 0%

commit v1 on v0

--- a/solution.py
+++ b/solution.py
@@ -64,7 +64,9 @@
     activated = jax.nn.elu(pre_act).astype(jnp.bfloat16)
     elu_slope = jnp.where(pre_act > 0, 1.0, jnp.exp(jnp.minimum(pre_act, 0.0)))
     dpre = (d_out.astype(jnp.float32) * elu_slope).astype(jnp.bfloat16)
-    dpre_group = lax.all_gather(dpre, "feat", axis=0, tiled=True)
+    dpre_group = jnp.concatenate(
+        lax.all_to_all(jnp.stack([dpre] * lax.axis_size("feat")), "feat", 0, 0), axis=0
+    )
     part_self = lax.dot_general(
         own_rows, dpre_group, (((0,), (0,)), ((), ())), preferred_element_type=jnp.float32
     )

time: 592 us -> 614 us (1.037)
  blocking collectives: 14.9 us -> 123 us
  waiting for transfers between devices: 245 us -> 161 us
    all_to_all x0 -> x1, blocking collectives: none -> 108 us  [shards(): lax.all_to_all(jnp.stack([dpre] * lax.axis_size('feat')), 'feat', 0, 0)]
    all_gather x1 -> x0, waiting for transfers between devices: 84.5 us -> none  [shards(): dpre_group = lax.all_gather(dpre, 'feat', axis=0, tiled=True)]
  transfers between devices with their start and end apart: 3 -> 2, of which waited for: 3 -> 2; matrix products, arithmetic and copies ran while one was open for 1% -> 1% of each run, Pallas kernels for 0% -> 0%
where the time goes in v1:
time: 614 us; the launch traced here: 609 us
  other arithmetic  209 us (34%)
  waiting for transfers between devices  161 us (26%)
  blocking collectives  123 us (20%)
  local copies, waits for them, and re-layouts  57.5 us (9%)
  matrix products  43.5 us (7%)
  between operations  14.1 us (2%)
    reduce_scatter x1, waiting for transfers between devices, shards(): lax.psum_scatter(jnp.dot(own_rows, w_self, preferred_element_type=jnp.flo...  151 us
    scatter-add x16, other arithmetic, backward_slot(): return grad_all.at[block_ids].add(product * live_mask[:, None, None])  120 us
    all_to_all x1, blocking collectives, shards(): lax.all_to_all(jnp.stack([dpre] * lax.axis_size('feat')), 'feat', 0, 0)  108 us
    shift_right_arithmetic x96, local copies, waits for them, and re-layouts, unpack(): jnp.right_shift(packed[..., :, None, :], shifts[:, None])  33.8 us
    convert_element_type x32, other arithmetic, slot_tiles(): adjacency = unpack(packed).astype(jnp.bfloat16)  23.8 us
    convert_element_type x32, other arithmetic, slot_tiles(): live_mask = (slot_idx < nbr_count).astype(jnp.float32)  21.2 us
    dot_general x16, matrix products, forward_slot(): jnp.einsum('bij,bjc->bic', adjacency, source, preferred_element_type=jnp....  19.2 us
    reduce_sum x16, other arithmetic, forward_slot(): jnp.sum(adjacency, axis=2, dtype=jnp.float32) * live_mask[:, None]  18.5 us
  transfers between devices with their start and end apart: 2, of which 2 were waited for; matrix products, arithmetic and copies ran while one was open for 1% of the time, Pallas kernels for 0%

profile of v1, /device:TPU:1, one launch (start us, length us, event | category | flops | bytes accessed | tf_op | source)
XLA Modules:
  0.0 608.5 jit_solution(3825650630199922125)
XLA Ops:
  8.6 4.6 copy.24
  13.1 101.6 %while.30 = (s32[]{:T(128)}, f32[64,128,16]{1,2,0:T(8,128)S(1)}, f32[64,128]{0,1:T(8,128)S(1)}, s32[64,16,8,128]{3,2,0,1:T(8,128)}, s32[64,16]{0,1:T(8,128)}, /*...) while((s32[]{:T(128)}, f32[64,128,16]{1,2,0:T(8,128)S(1)}, ...), condition=%wide.region_2.3_spmd.clone, body=%wide.region_0.2_spmd.clone.sunk | while | flops 42353984 | bytes 7282812 | solution.py:42
  18.3 1.2 fusion.61
  24.6 1.2 fusion.61
  114.9 1.3 fusion.18
  116.2 4.5 convolution_add_fusion
  120.8 150.8 %reduce-scatter.3.cloned.1.call-done = f32[128,256]{1,0:T(8,128)} async-done(((f32[8192,256]{1,0:T(8,128)}), f32[128,256]{1,0:T(8,128)}) %reduce-scatter.3.cloned.1.call-update) | async-done | bytes 131088 | tf_op jit(solution)/shard_map/reduce_scatter | solution.py:55
  271.6 1.6 fusion.23
  273.7 108.3 %all_to_all.5 = bf16[64,128,256]{2,1,0:T(8,128)(2,1)S(1)} all-to-all(bf16[64,128,256]{2,1,0:T(8,128)(2,1)S(1)} %stack.2), channel_id=1, replica_groups=mesh['feat'=64,'node'=4] {'feat'}, dimensions={0} | all-to-all | bytes 8388608 | tf_op jit(solution)/shard_map/all_to_all | solution.py:68
  383.3 1.5 broadcast_in_dim.47
  384.8 181.3 %while.29 = (s32[]{:T(128)}, f32[256,128,16]{1,2,0:T(8,128)}, s32[64,16]{0,1:T(8,128)}, s32[64,16,8,128]{3,2,0,1:T(8,128)}, bf16[64,128,16]{1,2,0:T(8,128)(2,1)S(1)}, /*index=5*/s32[64]{0:T(128)}, s32[]{:T(128)}) while((s32[]{:T(128)}, f32[256,128,16]{1,2,0:T(8,128)}, s32[64,16]{0,1:T(8,128)}, s32[64,16,8,128]{3,2,0,1:T(8,128)}, ...), condition=%wide.region_6.7_spmd, body=%wide.region_4.6_spmd.sunk | while | flops 36962624 | bytes 7343713 | solution.py:97
  388.6 7.5 %scatter_fusion = f32[256,128,16]{1,2,0:T(8,128)} fusion(f32[256,128,16]{1,2,0:T(8,128)} %get-tuple-element.451, s32[64]{0:T(128)S(1)} %fusion.55, f32[64,128,16]{1,2,0:T(8,128)S(1)} %convolution_multiply_fusion.3), kind=kCustom, calls=%fused_computation.1.clone.1 | custom fusion | flops 131072 | bytes 1573120 | tf_op jit(solution)/shard_map/while/body/eval_jaxpr/scatter-add | solution.py:95
  399.9 7.5 %scatter_fusion = f32[256,128,16]{1,2,0:T(8,128)} fusion(f32[256,128,16]{1,2,0:T(8,128)} %get-tuple-element.451, s32[64]{0:T(128)S(1)} %fusion.55, f32[64,128,16]{1,2,0:T(8,128)S(1)} %convolution_multiply_fusion.3), kind=kCustom, calls=%fused_computation.1.clone.1 | custom fusion | flops 131072 | bytes 1573120 | tf_op jit(solution)/shard_map/while/body/eval_jaxpr/scatter-add | solution.py:95
  411.3 7.5 %scatter_fusion = f32[256,128,16]{1,2,0:T(8,128)} fusion(f32[256,128,16]{1,2,0:T(8,128)} %get-tuple-element.451, s32[64]{0:T(128)S(1)} %fusion.55, f32[64,128,16]{1,2,0:T(8,128)S(1)} %convolution_multiply_fusion.3), kind=kCustom, calls=%fused_computation.1.clone.1 | custom fusion | flops 131072 | bytes 1573120 | tf_op jit(solution)/shard_map/while/body/eval_jaxpr/scatter-add | solution.py:95
  422.6 7.5 %scatter_fusion = f32[256,128,16]{1,2,0:T(8,128)} fusion(f32[256,128,16]{1,2,0:T(8,128)} %get-tuple-element.451, s32[64]{0:T(128)S(1)} %fusion.55, f32[64,128,16]{1,2,0:T(8,128)S(1)} %convolution_multiply_fusion.3), kind=kCustom, calls=%fused_computation.1.clone.1 | custom fusion | flops 131072 | bytes 1573120 | tf_op jit(solution)/shard_map/while/body/eval_jaxpr/scatter-add | solution.py:95
  433.9 7.5 %scatter_fusion = f32[256,128,16]{1,2,0:T(8,128)} fusion(f32[256,128,16]{1,2,0:T(8,128)} %get-tuple-element.451, s32[64]{0:T(128)S(1)} %fusion.55, f32[64,128,16]{1,2,0:T(8,128)S(1)} %convolution_multiply_fusion.3), kind=kCustom, calls=%fused_computation.1.clone.1 | custom fusion | flops 131072 | bytes 1573120 | tf_op jit(solution)/shard_map/while/body/eval_jaxpr/scatter-add | solution.py:95
  445.3 7.5 %scatter_fusion = f32[256,128,16]{1,2,0:T(8,128)} fusion(f32[256,128,16]{1,2,0:T(8,128)} %get-tuple-element.451, s32[64]{0:T(128)S(1)} %fusion.55, f32[64,128,16]{1,2,0:T(8,128)S(1)} %convolution_multiply_fusion.3), kind=kCustom, calls=%fused_computation.1.clone.1 | custom fusion | flops 131072 | bytes 1573120 | tf_op jit(solution)/shard_map/while/body/eval_jaxpr/scatter-add | solution.py:95
  456.6 7.5 %scatter_fusion = f32[256,128,16]{1,2,0:T(8,128)} fusion(f32[256,128,16]{1,2,0:T(8,128)} %get-tuple-element.451, s32[64]{0:T(128)S(1)} %fusion.55, f32[64,128,16]{1,2,0:T(8,128)S(1)} %convolution_multiply_fusion.3), kind=kCustom, calls=%fused_computation.1.clone.1 | custom fusion | flops 131072 | bytes 1573120 | tf_op jit(solution)/shard_map/while/body/eval_jaxpr/scatter-add | solution.py:95
  467.9 7.5 %scatter_fusion = f32[256,128,16]{1,2,0:T(8,128)} fusion(f32[256,128,16]{1,2,0:T(8,128)} %get-tuple-element.451, s32[64]{0:T(128)S(1)} %fusion.55, f32[64,128,16]{1,2,0:T(8,128)S(1)} %convolution_multiply_fusion.3), kind=kCustom, calls=%fused_computation.1.clone.1 | custom fusion | flops 131072 | bytes 1573120 | tf_op jit(solution)/shard_map/while/body/eval_jaxpr/scatter-add | solution.py:95
  479.3 7.5 %scatter_fusion = f32[256,128,16]{1,2,0:T(8,128)} fusion(f32[256,128,16]{1,2,0:T(8,128)} %get-tuple-element.451, s32[64]{0:T(128)S(1)} %fusion.55, f32[64,128,16]{1,2,0:T(8,128)S(1)} %convolution_multiply_fusion.3), kind=kCustom, calls=%fused_computation.1.clone.1 | custom fusion | flops 131072 | bytes 1573120 | tf_op jit(solution)/shard_map/while/body/eval_jaxpr/scatter-add | solution.py:95
  490.6 7.5 %scatter_fusion = f32[256,128,16]{1,2,0:T(8,128)} fusion(f32[256,128,16]{1,2,0:T(8,128)} %get-tuple-element.451, s32[64]{0:T(128)S(1)} %fusion.55, f32[64,128,16]{1,2,0:T(8,128)S(1)} %convolution_multiply_fusion.3), kind=kCustom, calls=%fused_computation.1.clone.1 | custom fusion | flops 131072 | bytes 1573120 | tf_op jit(solution)/shard_map/while/body/eval_jaxpr/scatter-add | solution.py:95
  501.9 7.5 %scatter_fusion = f32[256,128,16]{1,2,0:T(8,128)} fusion(f32[256,128,16]{1,2,0:T(8,128)} %get-tuple-element.451, s32[64]{0:T(128)S(1)} %fusion.55, f32[64,128,16]{1,2,0:T(8,128)S(1)} %convolution_multiply_fusion.3), kind=kCustom, calls=%fused_computation.1.clone.1 | custom fusion | flops 131072 | bytes 1573120 | tf_op jit(solution)/shard_map/while/body/eval_jaxpr/scatter-add | solution.py:95
  513.3 7.5 %scatter_fusion = f32[256,128,16]{1,2,0:T(8,128)} fusion(f32[256,128,16]{1,2,0:T(8,128)} %get-tuple-element.451, s32[64]{0:T(128)S(1)} %fusion.55, f32[64,128,16]{1,2,0:T(8,128)S(1)} %convolution_multiply_fusion.3), kind=kCustom, calls=%fused_computation.1.clone.1 | custom fusion | flops 131072 | bytes 1573120 | tf_op jit(solution)/shard_map/while/body/eval_jaxpr/scatter-add | solution.py:95
  524.6 7.5 %scatter_fusion = f32[256,128,16]{1,2,0:T(8,128)} fusion(f32[256,128,16]{1,2,0:T(8,128)} %get-tuple-element.451, s32[64]{0:T(128)S(1)} %fusion.55, f32[64,128,16]{1,2,0:T(8,128)S(1)} %convolution_multiply_fusion.3), kind=kCustom, calls=%fused_computation.1.clone.1 | custom fusion | flops 131072 | bytes 1573120 | tf_op jit(solution)/shard_map/while/body/eval_jaxpr/scatter-add | solution.py:95
  535.9 7.5 %scatter_fusion = f32[256,128,16]{1,2,0:T(8,128)} fusion(f32[256,128,16]{1,2,0:T(8,128)} %get-tuple-element.451, s32[64]{0:T(128)S(1)} %fusion.55, f32[64,128,16]{1,2,0:T(8,128)S(1)} %convolution_multiply_fusion.3), kind=kCustom, calls=%fused_computation.1.clone.1 | custom fusion | flops 131072 | bytes 1573120 | tf_op jit(solution)/shard_map/while/body/eval_jaxpr/scatter-add | solution.py:95
  547.2 7.5 %scatter_fusion = f32[256,128,16]{1,2,0:T(8,128)} fusion(f32[256,128,16]{1,2,0:T(8,128)} %get-tuple-element.451, s32[64]{0:T(128)S(1)} %fusion.55, f32[64,128,16]{1,2,0:T(8,128)S(1)} %convolution_multiply_fusion.3), kind=kCustom, calls=%fused_computation.1.clone.1 | custom fusion | flops 131072 | bytes 1573120 | tf_op jit(solution)/shard_map/while/body/eval_jaxpr/scatter-add | solution.py:95
  558.6 7.5 %scatter_fusion = f32[256,128,16]{1,2,0:T(8,128)} fusion(f32[256,128,16]{1,2,0:T(8,128)} %get-tuple-element.451, s32[64]{0:T(128)S(1)} %fusion.55, f32[64,128,16]{1,2,0:T(8,128)S(1)} %convolution_multiply_fusion.3), kind=kCustom, calls=%fused_computation.1.clone.1 | custom fusion | flops 131072 | bytes 1573120 | tf_op jit(solution)/shard_map/while/body/eval_jaxpr/scatter-add | solution.py:95
  566.1 3.2 copy_bitcast_fusion
  569.3 3.0 fusion.10
  572.3 3.0 fusion.16
  576.4 15.0 %all-reduce = (f32[16,256]{1,0:T(8,128)S(1)}, f32[16,256]{1,0:T(8,128)S(1)}) all-reduce(f32[16,256]{1,0:T(8,128)S(1)} %fusion.16, f32[16,256]{1,0:T(8,128)S(1)} %convolution_bitcast_fusion), channel_id=1, replica_groups=mesh['feat'=64,'node'=4] {'node'}, use_global_device_ids=true, to_apply=%region_8.9 | all-reduce | flops 8192 | bytes 65536 | tf_op jit(solution)/shard_map/psum | solution.py:76
  592.0 9.6 %reduce-scatter.5.cloned.1.call-done = f32[8192,16]{0,1:T(8,128)} async-done(((f32[32768,16]{0,1:T(8,128)}), f32[8192,16]{0,1:T(8,128)}) %reduce-scatter.5.cloned.1.call-update) | async-done | bytes 524304 | tf_op jit(solution)/shard_map/reduce_scatter | solution.py:105
  (332 shorter events, 164.5 us)
Async XLA Ops:
  7.2 1.2 copy-start
  7.2 264.4 %reduce-scatter.3.cloned.1.call-start = ((), (), s32[]{:S(2)}) async-start(), calls=%async_computation.3 | async-start | bytes 8519680 | tf_op jit(solution)/shard_map/reduce_scatter | solution.py:55
  13.1 101.7 %copy-start.6 = (bf16[16,256]{1,0:T(8,128)(2,1)S(1)}, bf16[16,256]{1,0:T(8,128)(2,1)}, u32[]{:S(2)}) copy-start(bf16[16,256]{1,0:T(8,128)(2,1)} %param.13) | copy-start | bytes 24580
  114.8 1.3 copy-start.5
  120.7 150.9 %copy-start.4 = (bf16[128,256]{1,0:T(8,128)(2,1)S(1)}, bf16[128,256]{1,0:T(8,128)(2,1)}, u32[]{:S(2)}) copy-start(bf16[128,256]{1,0:T(8,128)(2,1)} %param.16) | copy-start | bytes 196612
  120.7 150.9 %copy-start.7 = (f32[256]{0:T(256)S(1)}, f32[256]{0:T(256)}, u32[]{:S(2)}) copy-start(f32[256]{0:T(256)} %param.15) | copy-start | bytes 3076
  120.7 481.0 %reduce-scatter.5.cloned.1.call-start = ((), (), s32[]{:S(2)}) async-start(), calls=%async_computation.4 | async-start | bytes 2621440 | tf_op jit(solution)/shard_map/reduce_scatter | solution.py:105
  382.0 2.7 copy-start.1
  566.1 3.2 copy-start.2
  572.3 3.5 copy-start.3
Sparse Core Ops, SparseCore 0:
  120.8 150.7 reduce-scatter.2
  572.4 29.2 reduce-scatter.4
